TPU v7x, 32 devices: a whole 2x2x4 slice. The times are simulated.
32 devices in a mesh: ctx: 8 (over z, y), ch: 4 (over x, core).
Axes of the slice: x: 2, y: 2, z: 4, core: 2. Of those that a mesh axis runs over, the one named last changes fastest.
Arguments:
- tokens: bfloat16 [8192, 1536], P('ctx', 'ch'), may hold values from -6 to 6
- block_first: bfloat16 [16, 512, 512], P('ctx'), may hold values from -0.25 to 0.25
- block_second: bfloat16 [512, 16, 16], P('ctx'), may hold values from -1.5 to 1.5
- gate_weight: bfloat16 [1536, 1536], P(None, 'ch'), may hold values from -0.15625 to 0.15625
- conv_taps: float32 [4, 1536], P(None, 'ch'), may hold values from -3 to 3
- cotangent: bfloat16 [8192, 1536], P('ctx', 'ch'), may hold values from -6 to 6
Outputs:
- mixed_out: bfloat16 [8192, 1536], P('ctx', 'ch')
- grad_tokens: bfloat16 [8192, 1536], P('ctx', 'ch')
- grad_taps: float32 [4, 1536], P(None, 'ch')
- grad_gate_weight: float32 [1536, 1536], P(None, 'ch')
- grad_first: float32 [16, 512, 512], P('ctx')
- grad_second: float32 [512, 16, 16], P('ctx')
All inputs are finite; a program needn't handle non-finite values.
Results may differ from a plain program's by a relative error of at most 0.0064.
Values may be sent and summed in bfloat16 or wider, within the bound.
No kernel may reach another device: no remote copies, remote signals or barrier semaphores. Data moves between devices by JAX's collectives and lax.ppermute only.
A program may use at most 64 MiB of HBM per device.

v0:
```python
import jax
import jax.numpy as jnp
from jax import lax
from jax.sharding import PartitionSpec as P


def passed_along(array, axis, by):
    count = lax.axis_size(axis)
    pairs = [(i, i + by) for i in range(count) if 0 <= i + by < count]
    return lax.ppermute(array, axis, pairs)


def on_device(tokens, block_first, block_second, gate_weight, conv_taps, cotangent):
    blocks = block_first.shape[0]
    block_size = block_first.shape[1]
    tok_rows = tokens.shape[0]
    chan_count = tokens.shape[1]
    tap_count = conv_taps.shape[0]
    local_blocks = tokens.reshape(blocks, block_size, chan_count)
    first_out = jnp.einsum(
        "nrs,nsc->nrc", block_first, local_blocks, preferred_element_type=jnp.float32
    ).astype(jnp.bfloat16)
    columns = lax.all_to_all(first_out, "ctx", split_axis=1, concat_axis=0, tiled=True)
    second_out = jnp.einsum(
        "rmn,nrc->mrc", block_second, columns, preferred_element_type=jnp.float32
    ).astype(jnp.bfloat16)
    mixed_seq = lax.all_to_all(second_out, "ctx", split_axis=0, concat_axis=1, tiled=True).reshape(
        tok_rows, chan_count
    )
    features = lax.all_gather(tokens, "ch", axis=1, tiled=True)
    gate_pre = jnp.dot(features, gate_weight, preferred_element_type=jnp.float32)
    gate_sig = jax.nn.sigmoid(gate_pre)
    mixed_wide = mixed_seq.astype(jnp.float32)
    gated_vals = (mixed_wide * gate_sig).astype(jnp.bfloat16)
    earlier = passed_along(gated_vals[tok_rows - (tap_count - 1) :], "ctx", 1)
    padded = jnp.concatenate([earlier, gated_vals], 0).astype(jnp.float32)
    conv_out = jnp.zeros((tok_rows, chan_count), jnp.float32)
    for offset in range(tap_count):
        conv_out = (
            conv_out
            + conv_taps[offset][None, :]
            * padded[tap_count - 1 - offset : tap_count - 1 - offset + tok_rows]
        )
    mixed_out = conv_out.astype(jnp.bfloat16)
    following = passed_along(cotangent[: tap_count - 1], "ctx", -1)
    cot_wide = cotangent.astype(jnp.float32)
    cot_pad = jnp.concatenate([cotangent, following], 0).astype(jnp.float32)
    grad_gated = jnp.zeros((tok_rows, chan_count), jnp.float32)
    tap_rows = []
    for offset in range(tap_count):
        grad_gated = grad_gated + conv_taps[offset][None, :] * cot_pad[offset : offset + tok_rows]
        tap_rows.append(
            jnp.sum(
                cot_wide * padded[tap_count - 1 - offset : tap_count - 1 - offset + tok_rows], 0
            )
        )
    tap_part = jnp.stack(tap_rows, 0)
    grad_mix = (grad_gated * gate_sig).astype(jnp.bfloat16)
    grad_gate = (grad_gated * mixed_wide * gate_sig * (1.0 - gate_sig)).astype(jnp.bfloat16)
    weight_part = lax.dot_general(
        features, grad_gate, (((0,), (0,)), ((), ())), preferred_element_type=jnp.float32
    )
    grad_taps, grad_gate_weight = lax.psum((tap_part, weight_part), "ctx")
    full_part = lax.dot_general(
        grad_gate, gate_weight, (((1,), (1,)), ((), ())), preferred_element_type=jnp.float32
    )
    gate_input_grad = lax.psum_scatter(
        full_part.astype(jnp.bfloat16), "ch", scatter_dimension=1, tiled=True
    ).astype(jnp.float32)
    grad_cols = lax.all_to_all(
        grad_mix.reshape(blocks, block_size, chan_count),
        "ctx",
        split_axis=1,
        concat_axis=0,
        tiled=True,
    )
    second_part = jnp.einsum("mrc,nrc->rmn", grad_cols, columns, preferred_element_type=jnp.float32)
    grad_first_t = jnp.einsum(
        "rmn,mrc->nrc", block_second, grad_cols, preferred_element_type=jnp.float32
    ).astype(jnp.bfloat16)
    grad_back = lax.all_to_all(grad_first_t, "ctx", split_axis=0, concat_axis=1, tiled=True)
    first_part = jnp.einsum(
        "nrc,nsc->nrs", grad_back, local_blocks, preferred_element_type=jnp.float32
    )
    grad_local = jnp.einsum(
        "nrs,nrc->nsc", block_first, grad_back, preferred_element_type=jnp.float32
    ).reshape(tok_rows, chan_count)
    grad_tokens = (grad_local + gate_input_grad).astype(jnp.bfloat16)
    grad_first, grad_second = lax.psum((first_part, second_part), "ch")
    return (mixed_out, grad_tokens, grad_taps, grad_gate_weight, grad_first, grad_second)


def solution(mesh):
    in_specs = (
        P("ctx", "ch"),
        P("ctx", None, None),
        P("ctx", None, None),
        P(None, "ch"),
        P(None, "ch"),
        P("ctx", "ch"),
    )
    out_specs = (
        P("ctx", "ch"),
        P("ctx", "ch"),
        P(None, "ch"),
        P(None, "ch"),
        P("ctx", None, None),
        P("ctx", None, None),
    )
    return jax.shard_map(
        on_device, mesh=mesh, in_specs=in_specs, out_specs=out_specs, check_vma=False
    )
```

profile of v0, /device:TPU:0, one launch (start us, length us, event | category | flops | bytes accessed | tf_op | source)
XLA Modules:
  0.0 322.3 jit_solution(4741320819189164294)
XLA Ops:
  7.9 2.2 convolution_convert_fusion.1
  11.8 7.3 %all-to-all-start = ((bf16[2,512,384]{2,0,1:T(2,128)(2,1)}), bf16[2,512,384]{2,0,1:T(2,128)(2,1)S(1)}, u32[]{:S(2)}, u32[]{:S(2)}) async-start(bf16[2,512,384]{2,0,1:T(2,128)(2,1)} %copy.44), calls=%async_computation | async-start | bytes 1572864 | tf_op jit(solution)/shard_map/all_to_all | solution.py:23
  20.1 19.2 %all-to-all-done = bf16[2,512,384]{2,0,1:T(2,128)(2,1)S(1)} async-done(((bf16[2,512,384]{2,0,1:T(2,128)(2,1)}), bf16[2,512,384]{2,0,1:T(2,128)(2,1)S(1)}, u32[]{:S(2)}, u32[]{:S(2)}) %all-to-all-start) | async-done | bytes 786464 | tf_op jit(solution)/shard_map/all_to_all | solution.py:23
  42.3 3.6 %all-to-all-start.1 = ((bf16[16,64,384]{2,1,0:T(8,128)(2,1)}), bf16[16,64,384]{2,1,0:T(8,128)(2,1)S(1)}, u32[]{:S(2)}, u32[]{:S(2)}) async-start(bf16[16,64,384]{2,1,0:T(8,128)(2,1)} %copy.47), calls=%async_computation.1 | async-start | bytes 1572864 | tf_op jit(solution)/shard_map/all_to_all | solution.py:27
  48.0 4.0 %collective-permute-done.1 = bf16[3,384]{1,0:T(4,128)(2,1)S(1)} collective-permute-done((bf16[3,384]{1,0:T(4,128)(2,1)S(1)}, bf16[3,384]{1,0:T(4,128)(2,1)S(1)}, u32[]{:S(2)}, u32[]{:S(2)}) %collective-permute-start.1) | collective-permute-done | bytes 2336 | tf_op jit(solution)/shard_map/ppermute | solution.py:10
  53.3 13.0 %all-to-all-done.1 = bf16[16,64,384]{2,1,0:T(8,128)(2,1)S(1)} async-done(((bf16[16,64,384]{2,1,0:T(8,128)(2,1)}), bf16[16,64,384]{2,1,0:T(8,128)(2,1)S(1)}, u32[]{:S(2)}, u32[]{:S(2)}) %all-to-all-start.1) | async-done | bytes 786464 | tf_op jit(solution)/shard_map/all_to_all | solution.py:27
  67.6 8.1 %fusion.10 = (bf16[1024,384]{1,0:T(8,128)(2,1)}, f32[1024,384]{1,0:T(8,128)S(1)}, bf16[1024,384]{1,0:T(8,128)(2,1)}, f32[1024,384]{1,0:T(8,128)S(1)}) fusion(f32[8,2,64,384]{3,2,0,1:T(8,128)} %copy.48, f32[1027,384]{1,0:T(8,128)} %maximum_convert_fusion.1, f32[384]{0:T(512)S(1)} %get-tuple-element.36, f32[384]{0:T(512)S(1)} %get-tuple-element.37, ...), kind=kOutput, calls=%fused_computation.22 | convolution fusion | flops 1214644224 | bytes 16914432 | tf_op jit(solution)/shard_map/dot_general | solution.py:31
  77.6 4.0 %all-to-all-start.2 = ((bf16[2,512,384]{2,0,1:T(2,128)(2,1)}), bf16[2,512,384]{2,0,1:T(2,128)(2,1)S(1)}, u32[]{:S(2)}, u32[]{:S(2)}) async-start(bf16[2,512,384]{2,0,1:T(2,128)(2,1)} %copy.49), calls=%async_computation.2 | async-start | bytes 1572864 | tf_op jit(solution)/shard_map/all_to_all | solution.py:70
  81.6 5.0 %convolution_bitcast_fusion = f32[1536,384]{0,1:T(8,128)} fusion(bf16[1024,384]{1,0:T(8,128)(2,1)} %get-tuple-element.40, bf16[1024,1536]{1,0:T(8,128)(2,1)} %all-gather.2.cloned.1.call-done), kind=kOutput, calls=%fused_computation.1 | convolution fusion | flops 1207959552 | bytes 6291456 | tf_op jit(solution)/shard_map/dot_general | solution.py:60
  86.6 28.1 %all-to-all-done.2 = bf16[2,512,384]{2,0,1:T(2,128)(2,1)S(1)} async-done(((bf16[2,512,384]{2,0,1:T(2,128)(2,1)}), bf16[2,512,384]{2,0,1:T(2,128)(2,1)S(1)}, u32[]{:S(2)}, u32[]{:S(2)}) %all-to-all-start.2) | async-done | bytes 786464 | tf_op jit(solution)/shard_map/all_to_all | solution.py:70
  116.1 2.3 all_to_all.54
  120.8 4.2 %all-to-all-start.3 = ((bf16[16,64,384]{2,1,0:T(8,128)(2,1)}), bf16[16,64,384]{2,1,0:T(8,128)(2,1)}, u32[]{:S(2)}, u32[]{:S(2)}) async-start(bf16[16,64,384]{2,1,0:T(8,128)(2,1)} %copy.52), calls=%async_computation.3 | async-start | bytes 1572864 | tf_op jit(solution)/shard_map/all_to_all | solution.py:81
  126.4 20.1 %all-to-all-done.3 = bf16[16,64,384]{2,1,0:T(8,128)(2,1)} async-done(((bf16[16,64,384]{2,1,0:T(8,128)(2,1)}), bf16[16,64,384]{2,1,0:T(8,128)(2,1)}, u32[]{:S(2)}, u32[]{:S(2)}) %all-to-all-start.3) | async-done | bytes 786464 | tf_op jit(solution)/shard_map/all_to_all | solution.py:81
  147.7 2.1 fusion.15
  150.9 3.5 %convolution_convert_fusion = bf16[1024,1536]{1,0:T(8,128)(2,1)} fusion(bf16[1024,384]{1,0:T(8,128)(2,1)S(1)} %copy-done.7, bf16[1536,384]{1,0:T(8,128)(2,1)S(1)} %copy-done), kind=kOutput, calls=%fused_computation | convolution fusion | flops 1209532416 | bytes 5111808 | tf_op jit(solution)/shard_map/dot_general | solution.py:64
  154.4 4.6 %copy.59 = bf16[1024,1536]{0,1:T(8,128)(2,1)} copy(bf16[1024,1536]{1,0:T(8,128)(2,1)} %convolution_convert_fusion) | data formatting | bytes 6291456
  160.2 3.8 %collective-permute-start = (bf16[3,384]{1,0:T(4,128)(2,1)S(1)}, bf16[3,384]{1,0:T(4,128)(2,1)S(1)}, u32[]{:S(2)}, u32[]{:S(2)}) collective-permute-start(bf16[3,384]{1,0:T(4,128)(2,1)S(1)} %slice.64), channel_id=1, source_target_pairs={{0,4},{4,8},{8,12},{12,16},{16,20},{20,24},{24,28},{1,5},{5,9},{9,... | collective-permute-start | bytes 6920 | tf_op jit(solution)/shard_map/ppermute | solution.py:10
  165.6 2.1 fusion
  167.7 21.6 %psum.28 = f32[4,384]{1,0:T(4,128)} all-reduce(f32[4,384]{1,0:T(4,128)S(1)} %pad_maximum_fusion), channel_id=1, replica_groups=mesh['ctx'=8,'ch'=4] {'ctx'}, use_global_device_ids=true, to_apply=%region_5.0 | all-reduce | flops 1536 | bytes 12288 | tf_op jit(solution)/shard_map/psum | solution.py:63
  189.3 19.1 %all-reduce.4.cloned.1.call-done = f32[1536,384]{0,1:T(8,128)} async-done(((f32[1536,384]{0,1:T(8,128)}), f32[1536,384]{0,1:T(8,128)}) %all-reduce.4.cloned.1.call-update) | async-done | bytes 2359312 | tf_op jit(solution)/shard_map/psum | solution.py:63
  208.4 3.0 copy.56
  211.5 3.0 convolution_bitcast_fusion.1
  216.3 54.4 %all-reduce.6.cloned.1.call-done = (f32[2,512,512]{2,1,0:T(8,128)}, f32[64,16,16]{2,1,0:T(8,128)}) async-done(((f32[2,512,512]{2,1,0:T(8,128)}, f32[64,16,16]{2,1,0:T(8,128)}), (f32[2,512,512]{2,1,0:T(8,128)}, f32[64,16,16]{2,1,0:T(8,128)})) %all-reduce.6.cloned.1.call-update) | async-done | bytes 2162704 | tf_op jit(solution)/shard_map/psum | solution.py:89
  272.6 38.5 %reduce-scatter.4.cloned.1.call-done = bf16[384,1024]{1,0:T(8,128)(2,1)} async-done(((bf16[1536,1024]{1,0:T(8,128)(2,1)}), bf16[384,1024]{1,0:T(8,128)(2,1)}) %reduce-scatter.4.cloned.1.call-update) | async-done | bytes 786448
  (56 shorter events, 31.6 us)
Async XLA Ops:
  7.2 60.4 %copy-start = (bf16[1536,384]{1,0:T(8,128)(2,1)S(1)}, bf16[1536,384]{1,0:T(8,128)(2,1)}, u32[]{:S(2)}) copy-start(bf16[1536,384]{1,0:T(8,128)(2,1)} %param.9) | copy-start | bytes 3538948
  7.2 60.4 %all-gather.2.cloned.1.call-start = ((), (), s32[]{:S(2)}) async-start(), calls=%async_computation.5 | async-start | bytes 3932160 | tf_op jit(solution)/shard_map/all_gather | solution.py:30
  10.1 9.0 %copy-start.6 = (bf16[64,16,16]{0,2,1:T(8,128)(2,1)S(1)}, bf16[64,16,16]{0,2,1:T(8,128)(2,1)}, u32[]{:S(2)}) copy-start(bf16[64,16,16]{0,2,1:T(8,128)(2,1)} %param.8) | copy-start | bytes 98308
  11.8 27.5 %all-to-all-start = ((bf16[2,512,384]{2,0,1:T(2,128)(2,1)}), bf16[2,512,384]{2,0,1:T(2,128)(2,1)S(1)}, u32[]{:S(2)}, u32[]{:S(2)}) async-start(bf16[2,512,384]{2,0,1:T(2,128)(2,1)} %copy.44), calls=%async_computation | async-start | bytes 1572864 | tf_op jit(solution)/shard_map/all_to_all | solution.py:23
  39.8 1.0 copy-start.3
  41.2 4.6 %copy-start.1 = (bf16[1024,384]{1,0:T(8,128)(2,1)S(1)}, bf16[1024,384]{1,0:T(8,128)(2,1)}, u32[]{:S(2)}) copy-start(bf16[1024,384]{1,0:T(8,128)(2,1)} %param.11) | copy-start | bytes 2359300
  42.3 24.0 %all-to-all-start.1 = ((bf16[16,64,384]{2,1,0:T(8,128)(2,1)}), bf16[16,64,384]{2,1,0:T(8,128)(2,1)S(1)}, u32[]{:S(2)}, u32[]{:S(2)}) async-start(bf16[16,64,384]{2,1,0:T(8,128)(2,1)} %copy.47), calls=%async_computation.1 | async-start | bytes 1572864 | tf_op jit(solution)/shard_map/all_to_all | solution.py:27
  45.8 6.2 %collective-permute-start.1 = (bf16[3,384]{1,0:T(4,128)(2,1)S(1)}, bf16[3,384]{1,0:T(4,128)(2,1)S(1)}, u32[]{:S(2)}, u32[]{:S(2)}) collective-permute-start(bf16[3,384]{1,0:T(4,128)(2,1)S(1)} %slice.59), channel_id=1, source_target_pairs={{4,0},{8,4},{12,8},{16,12},{20,16},{24,20},{28,24},{5,1},{9,5},{13... | collective-permute-start | bytes 6920 | tf_op jit(solution)/shard_map/ppermute | solution.py:10
  77.6 37.1 %all-to-all-start.2 = ((bf16[2,512,384]{2,0,1:T(2,128)(2,1)}), bf16[2,512,384]{2,0,1:T(2,128)(2,1)S(1)}, u32[]{:S(2)}, u32[]{:S(2)}) async-start(bf16[2,512,384]{2,0,1:T(2,128)(2,1)} %copy.49), calls=%async_computation.2 | async-start | bytes 1572864 | tf_op jit(solution)/shard_map/all_to_all | solution.py:70
  81.6 126.8 %all-reduce.4.cloned.1.call-start = ((), (), s32[]{:S(2)}) async-start(), calls=%async_computation.6 | async-start | bytes 4718592 | tf_op jit(solution)/shard_map/psum | solution.py:63
  120.8 25.6 %all-to-all-start.3 = ((bf16[16,64,384]{2,1,0:T(8,128)(2,1)}), bf16[16,64,384]{2,1,0:T(8,128)(2,1)}, u32[]{:S(2)}, u32[]{:S(2)}) async-start(bf16[16,64,384]{2,1,0:T(8,128)(2,1)} %copy.52), calls=%async_computation.3 | async-start | bytes 1572864 | tf_op jit(solution)/shard_map/all_to_all | solution.py:81
  125.0 145.7 %all-reduce.6.cloned.1.call-start = ((), (), s32[]{:S(2)}) async-start(), calls=%async_computation.8 | async-start | bytes 5242880 | tf_op jit(solution)/shard_map/psum | solution.py:89
  126.4 21.3 %copy-start.2 = (bf16[1024,384]{1,0:T(8,128)(2,1)S(1)}, bf16[1024,384]{1,0:T(8,128)(2,1)}, u32[]{:S(2)}) copy-start(bf16[1024,384]{1,0:T(8,128)(2,1)} %param.6) | copy-start | bytes 2359300
  149.7 1.1 copy-start.7
  149.8 161.3 %reduce-scatter.4.cloned.1.call-start = ((), (), s32[]{:S(2)}) async-start(), calls=%async_computation.7 | async-start | bytes 3932160
  159.1 1.2 copy-start.5
  160.2 5.1 %collective-permute-start = (bf16[3,384]{1,0:T(4,128)(2,1)S(1)}, bf16[3,384]{1,0:T(4,128)(2,1)S(1)}, u32[]{:S(2)}, u32[]{:S(2)}) collective-permute-start(bf16[3,384]{1,0:T(4,128)(2,1)S(1)} %slice.64), channel_id=1, source_target_pairs={{0,4},{4,8},{8,12},{12,16},{16,20},{20,24},{24,28},{1,5},{5,9},{9,... | collective-permute-start | bytes 6920 | tf_op jit(solution)/shard_map/ppermute | solution.py:10
  312.6 1.9 copy-start.4
Sparse Core Ops, SparseCore 0:
  9.6 31.1 all-gather.1
  86.7 121.6 all-reduce.3
  211.5 59.1 all-reduce.5
  273.1 37.9 reduce-scatter.3
where the time goes:
time: 323 us; the launch traced here: 322 us
  waiting for transfers between devices  198 us (61%)
  local copies, waits for them, and re-layouts  32.2 us (10%)
  matrix products  26.9 us (8%)
  starting transfers between devices  24.6 us (8%)
  blocking collectives  21.6 us (7%)
  between operations  14 us (4%)
  other arithmetic  4.69 us (1%)
    psum x1, waiting for transfers between devices, on_device(): grad_first, grad_second = lax.psum((first_part, second_part), 'ch')  54.4 us
    unnamed x5, waiting for transfers between devices  39.2 us
    all_to_all x1, waiting for transfers between devices, on_device(): lax.all_to_all(grad_mix.reshape(blocks, block_size, chan_count), 'ctx', s...  28.1 us
    psum x1, blocking collectives, on_device(): grad_taps, grad_gate_weight = lax.psum((tap_part, weight_part), 'ctx')  21.6 us
    all_to_all x1, waiting for transfers between devices, on_device(): lax.all_to_all(grad_first_t, 'ctx', split_axis=0, concat_axis=1, tiled=True)  20.1 us
    all_to_all x1, waiting for transfers between devices, on_device(): lax.all_to_all(first_out, 'ctx', split_axis=1, concat_axis=0, tiled=True)  19.2 us
    psum x1, waiting for transfers between devices, on_device(): grad_taps, grad_gate_weight = lax.psum((tap_part, weight_part), 'ctx')  19.1 us
    unnamed x22, local copies, waits for them, and re-layouts  16.9 us
  transfers between devices with their start and end apart: 10, of which 9 were waited for; matrix products, arithmetic and copies ran while one was open for 14% of the time, Pallas kernels for 0%

commit v1 on v0

--- a/solution.py
+++ b/solution.py
@@ -67,13 +67,16 @@
     gate_input_grad = lax.psum_scatter(
         full_part.astype(jnp.bfloat16), "ch", scatter_dimension=1, tiled=True
     ).astype(jnp.float32)
-    grad_cols = lax.all_to_all(
-        grad_mix.reshape(blocks, block_size, chan_count),
-        "ctx",
-        split_axis=1,
-        concat_axis=0,
-        tiled=True,
-    )
+
+    def proceed_rounds_for(local_values, across):
+        return jnp.concatenate(
+            jax.lax.all_to_all(
+                jnp.stack(jnp.split(local_values, jax.lax.axis_size(across), 1)), across, 0, 0
+            ),
+            0,
+        )
+
+    grad_cols = proceed_rounds_for(grad_mix.reshape(blocks, block_size, chan_count), "ctx")
     second_part = jnp.einsum("mrc,nrc->rmn", grad_cols, columns, preferred_element_type=jnp.float32)
     grad_first_t = jnp.einsum(
         "rmn,mrc->nrc", block_second, grad_cols, preferred_element_type=jnp.float32

time: 323 us -> 331 us (1.025)
  waiting for transfers between devices: 198 us -> 207 us
    psum x1, waiting for transfers between devices: 19.1 us -> 27.3 us  [on_device(): grad_taps, grad_gate_weight = lax.psum((tap_part, weight_part), 'ctx')]
    unnamed x22 -> x29, local copies, waits for them, and re-layouts: 16.9 us -> 21.6 us
    all_to_all x2 -> x0, local copies, waits for them, and re-layouts: 3.69 us -> none  [on_device(): lax.all_to_all(grad_mix.reshape(blocks, block_size, chan_count), 'ctx', s...]
  transfers between devices with their start and end apart: 10 -> 10, of which waited for: 9 -> 9; matrix products, arithmetic and copies ran while one was open for 14% -> 13% of each run, Pallas kernels for 0% -> 0%
where the time goes in v1:
time: 331 us; the launch traced here: 330 us
  waiting for transfers between devices  207 us (63%)
  local copies, waits for them, and re-layouts  32.2 us (10%)
  matrix products  27.2 us (8%)
  starting transfers between devices  24 us (7%)
  blocking collectives  21.4 us (6%)
  between operations  14 us (4%)
  other arithmetic  4.69 us (1%)
    psum x1, waiting for transfers between devices, on_device(): grad_first, grad_second = lax.psum((first_part, second_part), 'ch')  54.3 us
    unnamed x5, waiting for transfers between devices  39.2 us
    all_to_all x1, waiting for transfers between devices, proceed_rounds_for(): jax.lax.all_to_all(jnp.stack(jnp.split(local_values, jax.lax.axis_size(ac...  28.1 us
    psum x1, waiting for transfers between devices, on_device(): grad_taps, grad_gate_weight = lax.psum((tap_part, weight_part), 'ctx')  27.3 us
    unnamed x29, local copies, waits for them, and re-layouts  21.6 us
    psum x1, blocking collectives, on_device(): grad_taps, grad_gate_weight = lax.psum((tap_part, weight_part), 'ctx')  21.4 us
    all_to_all x1, waiting for transfers between devices, on_device(): lax.all_to_all(grad_first_t, 'ctx', split_axis=0, concat_axis=1, tiled=True)  20.8 us
    all_to_all x1, waiting for transfers between devices, on_device(): lax.all_to_all(first_out, 'ctx', split_axis=1, concat_axis=0, tiled=True)  19.2 us
  transfers between devices with their start and end apart: 10, of which 9 were waited for; matrix products, arithmetic and copies ran while one was open for 13% of the time, Pallas kernels for 0%

profile of v1, /device:TPU:0, one launch (start us, length us, event | category | flops | bytes accessed | tf_op | source)
XLA Modules:
  0.0 330.3 jit_solution(500461419207449065)
XLA Ops:
  7.9 2.2 convolution_convert_fusion.1
  11.8 7.3 %all-to-all-start = ((bf16[2,512,384]{2,0,1:T(2,128)(2,1)}), bf16[2,512,384]{2,0,1:T(2,128)(2,1)S(1)}, u32[]{:S(2)}, u32[]{:S(2)}) async-start(bf16[2,512,384]{2,0,1:T(2,128)(2,1)} %copy.43), calls=%async_computation | async-start | bytes 1572864 | tf_op jit(solution)/shard_map/all_to_all | solution.py:23
  20.1 19.2 %all-to-all-done = bf16[2,512,384]{2,0,1:T(2,128)(2,1)S(1)} async-done(((bf16[2,512,384]{2,0,1:T(2,128)(2,1)}), bf16[2,512,384]{2,0,1:T(2,128)(2,1)S(1)}, u32[]{:S(2)}, u32[]{:S(2)}) %all-to-all-start) | async-done | bytes 786464 | tf_op jit(solution)/shard_map/all_to_all | solution.py:23
  42.3 3.6 %all-to-all-start.1 = ((bf16[16,64,384]{2,1,0:T(8,128)(2,1)}), bf16[16,64,384]{2,1,0:T(8,128)(2,1)S(1)}, u32[]{:S(2)}, u32[]{:S(2)}) async-start(bf16[16,64,384]{2,1,0:T(8,128)(2,1)} %copy.46), calls=%async_computation.1 | async-start | bytes 1572864 | tf_op jit(solution)/shard_map/all_to_all | solution.py:27
  48.0 4.0 %collective-permute-done.1 = bf16[3,384]{1,0:T(4,128)(2,1)S(1)} collective-permute-done((bf16[3,384]{1,0:T(4,128)(2,1)S(1)}, bf16[3,384]{1,0:T(4,128)(2,1)S(1)}, u32[]{:S(2)}, u32[]{:S(2)}) %collective-permute-start.1) | collective-permute-done | bytes 2336 | tf_op jit(solution)/shard_map/ppermute | solution.py:10
  53.3 13.0 %all-to-all-done.1 = bf16[16,64,384]{2,1,0:T(8,128)(2,1)S(1)} async-done(((bf16[16,64,384]{2,1,0:T(8,128)(2,1)}), bf16[16,64,384]{2,1,0:T(8,128)(2,1)S(1)}, u32[]{:S(2)}, u32[]{:S(2)}) %all-to-all-start.1) | async-done | bytes 786464 | tf_op jit(solution)/shard_map/all_to_all | solution.py:27
  67.6 8.1 %fusion.10 = (bf16[1024,384]{1,0:T(8,128)(2,1)}, f32[1024,384]{1,0:T(8,128)S(1)}, bf16[1024,384]{1,0:T(8,128)(2,1)}, f32[1024,384]{1,0:T(8,128)S(1)}) fusion(f32[8,2,64,384]{3,2,0,1:T(8,128)} %copy.47, f32[1027,384]{1,0:T(8,128)} %maximum_convert_fusion.1, f32[384]{0:T(512)S(1)} %get-tuple-element.36, f32[384]{0:T(512)S(1)} %get-tuple-element.37, ...), kind=kOutput, calls=%fused_computation.22 | convolution fusion | flops 1214644224 | bytes 16914432 | tf_op jit(solution)/shard_map/dot_general | solution.py:31
  81.1 4.0 %all-to-all-start.2 = ((bf16[8,2,64,384]{3,2,1,0:T(8,128)(2,1)}), bf16[8,2,64,384]{3,2,1,0:T(8,128)(2,1)S(1)}, u32[]{:S(2)}, u32[]{:S(2)}) async-start(bf16[8,2,64,384]{3,2,1,0:T(8,128)(2,1)} %fusion.17), calls=%async_computation.2 | async-start | bytes 1572864 | tf_op jit(solution)/shard_map/all_to_all | solution.py:73
  85.2 5.0 %convolution_bitcast_fusion = f32[1536,384]{0,1:T(8,128)} fusion(bf16[1024,384]{1,0:T(8,128)(2,1)} %get-tuple-element.40, bf16[1024,1536]{1,0:T(8,128)(2,1)} %all-gather.2.cloned.1.call-done), kind=kOutput, calls=%fused_computation.1 | convolution fusion | flops 1207959552 | bytes 6291456 | tf_op jit(solution)/shard_map/dot_general | solution.py:60
  90.1 28.1 %all-to-all-done.2 = bf16[8,2,64,384]{3,2,1,0:T(8,128)(2,1)S(1)} async-done(((bf16[8,2,64,384]{3,2,1,0:T(8,128)(2,1)}), bf16[8,2,64,384]{3,2,1,0:T(8,128)(2,1)S(1)}, u32[]{:S(2)}, u32[]{:S(2)}) %all-to-all-start.2) | async-done | bytes 786464 | tf_op jit(solution)/shard_map/all_to_all | solution.py:73
  120.8 4.2 %all-to-all-start.3 = ((bf16[16,64,384]{2,1,0:T(8,128)(2,1)}), bf16[16,64,384]{2,1,0:T(8,128)(2,1)}, u32[]{:S(2)}, u32[]{:S(2)}) async-start(bf16[16,64,384]{2,1,0:T(8,128)(2,1)} %copy.50), calls=%async_computation.3 | async-start | bytes 1572864 | tf_op jit(solution)/shard_map/all_to_all | solution.py:84
  126.5 20.8 %all-to-all-done.3 = bf16[16,64,384]{2,1,0:T(8,128)(2,1)} async-done(((bf16[16,64,384]{2,1,0:T(8,128)(2,1)}), bf16[16,64,384]{2,1,0:T(8,128)(2,1)}, u32[]{:S(2)}, u32[]{:S(2)}) %all-to-all-start.3) | async-done | bytes 786464 | tf_op jit(solution)/shard_map/all_to_all | solution.py:84
  148.5 2.1 fusion.26
  151.7 3.5 %convolution_convert_fusion = bf16[1024,1536]{1,0:T(8,128)(2,1)} fusion(bf16[1024,384]{1,0:T(8,128)(2,1)S(1)} %copy-done.7, bf16[1536,384]{1,0:T(8,128)(2,1)S(1)} %copy-done), kind=kOutput, calls=%fused_computation | convolution fusion | flops 1209532416 | bytes 5111808 | tf_op jit(solution)/shard_map/dot_general | solution.py:64
  155.2 4.7 %copy.58 = bf16[1024,1536]{0,1:T(8,128)(2,1)} copy(bf16[1024,1536]{1,0:T(8,128)(2,1)} %convolution_convert_fusion) | data formatting | bytes 6291456
  161.0 3.4 %collective-permute-start = (bf16[3,384]{1,0:T(4,128)(2,1)S(1)}, bf16[3,384]{1,0:T(4,128)(2,1)S(1)}, u32[]{:S(2)}, u32[]{:S(2)}) collective-permute-start(bf16[3,384]{1,0:T(4,128)(2,1)S(1)} %slice.64), channel_id=1, source_target_pairs={{0,4},{4,8},{8,12},{12,16},{16,20},{20,24},{24,28},{1,5},{5,9},{9,... | collective-permute-start | bytes 6920 | tf_op jit(solution)/shard_map/ppermute | solution.py:10
  165.7 2.1 fusion
  167.8 21.4 %psum.28 = f32[4,384]{1,0:T(4,128)} all-reduce(f32[4,384]{1,0:T(4,128)S(1)} %pad_maximum_fusion), channel_id=1, replica_groups=mesh['ctx'=8,'ch'=4] {'ctx'}, use_global_device_ids=true, to_apply=%region_5.0 | all-reduce | flops 1536 | bytes 12288 | tf_op jit(solution)/shard_map/psum | solution.py:63
  189.2 27.3 %all-reduce.4.cloned.1.call-done = f32[1536,384]{0,1:T(8,128)} async-done(((f32[1536,384]{0,1:T(8,128)}), f32[1536,384]{0,1:T(8,128)}) %all-reduce.4.cloned.1.call-update) | async-done | bytes 2359312 | tf_op jit(solution)/shard_map/psum | solution.py:63
  216.5 3.0 copy.54
  219.5 3.0 convolution_bitcast_fusion.1
  224.4 54.3 %all-reduce.6.cloned.1.call-done = (f32[2,512,512]{2,1,0:T(8,128)}, f32[64,16,16]{2,1,0:T(8,128)}) async-done(((f32[2,512,512]{2,1,0:T(8,128)}, f32[64,16,16]{2,1,0:T(8,128)}), (f32[2,512,512]{2,1,0:T(8,128)}, f32[64,16,16]{2,1,0:T(8,128)})) %all-reduce.6.cloned.1.call-update) | async-done | bytes 2162704 | tf_op jit(solution)/shard_map/psum | solution.py:92
  278.7 1.9 copy.55
  280.6 38.5 %reduce-scatter.4.cloned.1.call-done = bf16[384,1024]{1,0:T(8,128)(2,1)} async-done(((bf16[1536,1024]{1,0:T(8,128)(2,1)}), bf16[384,1024]{1,0:T(8,128)(2,1)}) %reduce-scatter.4.cloned.1.call-update) | async-done | bytes 786448
  (61 shorter events, 31.9 us)
Async XLA Ops:
  7.2 60.4 %copy-start = (bf16[1536,384]{1,0:T(8,128)(2,1)S(1)}, bf16[1536,384]{1,0:T(8,128)(2,1)}, u32[]{:S(2)}) copy-start(bf16[1536,384]{1,0:T(8,128)(2,1)} %param.9) | copy-start | bytes 3538948
  7.2 60.4 %all-gather.2.cloned.1.call-start = ((), (), s32[]{:S(2)}) async-start(), calls=%async_computation.5 | async-start | bytes 3932160 | tf_op jit(solution)/shard_map/all_gather | solution.py:30
  10.1 9.0 %copy-start.6 = (bf16[64,16,16]{0,2,1:T(8,128)(2,1)S(1)}, bf16[64,16,16]{0,2,1:T(8,128)(2,1)}, u32[]{:S(2)}) copy-start(bf16[64,16,16]{0,2,1:T(8,128)(2,1)} %param.8) | copy-start | bytes 98308
  11.8 27.5 %all-to-all-start = ((bf16[2,512,384]{2,0,1:T(2,128)(2,1)}), bf16[2,512,384]{2,0,1:T(2,128)(2,1)S(1)}, u32[]{:S(2)}, u32[]{:S(2)}) async-start(bf16[2,512,384]{2,0,1:T(2,128)(2,1)} %copy.43), calls=%async_computation | async-start | bytes 1572864 | tf_op jit(solution)/shard_map/all_to_all | solution.py:23
  39.8 1.0 copy-start.3
  41.2 4.6 %copy-start.1 = (bf16[1024,384]{1,0:T(8,128)(2,1)S(1)}, bf16[1024,384]{1,0:T(8,128)(2,1)}, u32[]{:S(2)}) copy-start(bf16[1024,384]{1,0:T(8,128)(2,1)} %param.11) | copy-start | bytes 2359300
  42.3 24.0 %all-to-all-start.1 = ((bf16[16,64,384]{2,1,0:T(8,128)(2,1)}), bf16[16,64,384]{2,1,0:T(8,128)(2,1)S(1)}, u32[]{:S(2)}, u32[]{:S(2)}) async-start(bf16[16,64,384]{2,1,0:T(8,128)(2,1)} %copy.46), calls=%async_computation.1 | async-start | bytes 1572864 | tf_op jit(solution)/shard_map/all_to_all | solution.py:27
  45.8 6.2 %collective-permute-start.1 = (bf16[3,384]{1,0:T(4,128)(2,1)S(1)}, bf16[3,384]{1,0:T(4,128)(2,1)S(1)}, u32[]{:S(2)}, u32[]{:S(2)}) collective-permute-start(bf16[3,384]{1,0:T(4,128)(2,1)S(1)} %slice.59), channel_id=1, source_target_pairs={{4,0},{8,4},{12,8},{16,12},{20,16},{24,20},{28,24},{5,1},{9,5},{13... | collective-permute-start | bytes 6920 | tf_op jit(solution)/shard_map/ppermute | solution.py:10
  81.1 37.1 %all-to-all-start.2 = ((bf16[8,2,64,384]{3,2,1,0:T(8,128)(2,1)}), bf16[8,2,64,384]{3,2,1,0:T(8,128)(2,1)S(1)}, u32[]{:S(2)}, u32[]{:S(2)}) async-start(bf16[8,2,64,384]{3,2,1,0:T(8,128)(2,1)} %fusion.17), calls=%async_computation.2 | async-start | bytes 1572864 | tf_op jit(solution)/shard_map/all_to_all | solution.py:73
  85.1 131.4 %all-reduce.4.cloned.1.call-start = ((), (), s32[]{:S(2)}) async-start(), calls=%async_computation.6 | async-start | bytes 4718592 | tf_op jit(solution)/shard_map/psum | solution.py:63
  120.8 26.5 %all-to-all-start.3 = ((bf16[16,64,384]{2,1,0:T(8,128)(2,1)}), bf16[16,64,384]{2,1,0:T(8,128)(2,1)}, u32[]{:S(2)}, u32[]{:S(2)}) async-start(bf16[16,64,384]{2,1,0:T(8,128)(2,1)} %copy.50), calls=%async_computation.3 | async-start | bytes 1572864 | tf_op jit(solution)/shard_map/all_to_all | solution.py:84
  125.0 153.7 %all-reduce.6.cloned.1.call-start = ((), (), s32[]{:S(2)}) async-start(), calls=%async_computation.8 | async-start | bytes 5242880 | tf_op jit(solution)/shard_map/psum | solution.py:92
  126.5 22.0 %copy-start.2 = (bf16[1024,384]{1,0:T(8,128)(2,1)S(1)}, bf16[1024,384]{1,0:T(8,128)(2,1)}, u32[]{:S(2)}) copy-start(bf16[1024,384]{1,0:T(8,128)(2,1)} %param.6) | copy-start | bytes 2359300
  150.6 1.1 copy-start.7
  150.6 168.5 %reduce-scatter.4.cloned.1.call-start = ((), (), s32[]{:S(2)}) async-start(), calls=%async_computation.7 | async-start | bytes 3932160
  159.9 1.1 copy-start.5
  161.0 4.6 %collective-permute-start = (bf16[3,384]{1,0:T(4,128)(2,1)S(1)}, bf16[3,384]{1,0:T(4,128)(2,1)S(1)}, u32[]{:S(2)}, u32[]{:S(2)}) collective-permute-start(bf16[3,384]{1,0:T(4,128)(2,1)S(1)} %slice.64), channel_id=1, source_target_pairs={{0,4},{4,8},{8,12},{12,16},{16,20},{20,24},{24,28},{1,5},{5,9},{9,... | collective-permute-start | bytes 6920 | tf_op jit(solution)/shard_map/ppermute | solution.py:10
  320.6 1.9 copy-start.4
Sparse Core Ops, SparseCore 0:
  9.6 31.1 all-gather.1
  90.3 126.1 all-reduce.3
  219.6 59.0 all-reduce.5
  281.1 37.9 reduce-scatter.3
